TPU v7x, 128 devices: a whole 4x4x4 slice. The times are simulated.
128 devices in a mesh: dp: 2 (over x_lo), space: 64 (over z, y, x_hi, core).
Axes of the slice: x: 4 (x_hi: 2, x_lo: 2; x = x_hi * 2 + x_lo), y: 4, z: 4, core: 2. Of those that a mesh axis runs over, the one named last changes fastest.
Arguments:
- stash: bfloat16 [64, 64, 4, 2160], P('space', None, 'dp'), may hold values from -5 to 5
- piece_map: int32 [64, 64], P(None, 'space'), may hold values from 0 to 63, as said below
- gain_one: float32 [768], replicated, may hold values from 0.5 to 1.5
- spec_one: float32 [2, 8, 96, 96], replicated, may hold values from -0.4375 to 0.4375
- bias_one: float32 [2, 768], replicated, may hold values from -3 to 3
- spec_two: float32 [2, 8, 96, 96], replicated, may hold values from -0.4375 to 0.4375
- bias_two: float32 [2, 768], replicated, may hold values from -0.6 to 0.6
- gain_two: float32 [768], replicated, may hold values from 0.5 to 1.5
- fc_one: bfloat16 [768, 3072], replicated, may hold values from -0.21875 to 0.21875
- bias_fc: float32 [3072], replicated, may hold values from -3 to 3
- fc_two: bfloat16 [3072, 768], replicated, may hold values from -0.109375 to 0.109375
- cotangent: bfloat16 [4, 64, 180, 768], P('dp', 'space'), may hold values from -6 to 6
Outputs:
- grad_input: float32 [4, 64, 180, 768], P('dp', 'space')
- grad_fc_one: float32 [768, 3072], P(None, ('dp', 'space'))
- grad_fc_two: float32 [3072, 768], P(('dp', 'space'))
- grad_bias_fc: float32 [3072], replicated
- grad_bias_out: float32 [768], replicated
- grad_gain_one: float32 [768], replicated
- grad_gain_two: float32 [768], replicated
- grad_spec_one: float32 [2, 8, 96, 96], replicated
- grad_bias_one: float32 [2, 768], replicated
- grad_spec_two: float32 [2, 8, 96, 96], replicated
- grad_bias_two: float32 [2, 768], replicated
Inputs may be any that keep to these rules, and one draw needn't show every extreme that they name: `piece_map`: each column holds every number from 0 to 63 once.
All inputs are finite; a program needn't handle non-finite values.
Results may differ from a plain program's by a relative error of at most 0.0046.
Values may be sent and summed in bfloat16 or wider, within the bound.
No kernel may reach another device: no remote copies, remote signals or barrier semaphores. Data moves between devices by JAX's collectives and lax.ppermute only.
A program may use at most 128 MiB of HBM per device.

v0:
```python
import math
import jax
import jax.numpy as jnp
from jax import lax
from jax.sharding import PartitionSpec as P

KW = 64
epsilon = 1e-05
highest = lax.Precision.HIGHEST


def in_one_piece(arrays, axis, split_dim, concat_dim, along):
    both = jnp.concatenate(arrays, axis=along)
    result, at, finished = (
        lax.all_to_all(both, axis, split_axis=split_dim, concat_axis=concat_dim, tiled=True),
        0,
        [],
    )
    for a in arrays:
        finished.append(lax.slice_in_dim(result, at, at + a.shape[along], axis=along))
        at += a.shape[along]
    return tuple(finished)


def side_by_side(arrays, axis, dim, along):
    widths = [a.shape[along] for a in arrays]
    both = jnp.concatenate(arrays, axis=along)
    result = lax.psum_scatter(both, axis, scatter_dimension=dim, tiled=True)
    return tuple(jnp.split(result, [sum(widths[:k]) for k in range(1, len(widths))], axis=along))


def layer_norm(values, gain_vector):
    centred = values - jnp.mean(values, axis=-1, keepdims=True)
    spread = jnp.mean(centred * centred, axis=-1, keepdims=True)
    return centred * lax.rsqrt(spread + epsilon) * gain_vector


def smooth_gate(values):
    return jax.nn.gelu(values, approximate=True)


def block_mix(real_part, imag_part, weights, biases):
    blocks = weights.shape[1]
    width_block = weights.shape[2]
    leading = real_part.shape[:-1]
    real_blocks = real_part.reshape(leading + (blocks, width_block))
    imag_blocks = imag_part.reshape(leading + (blocks, width_block))
    bias_real = biases[0].reshape(blocks, width_block)
    bias_imag = biases[1].reshape(blocks, width_block)
    new_real = (
        jnp.einsum("...ni,nio->...no", real_blocks, weights[0], precision=highest)
        - jnp.einsum("...ni,nio->...no", imag_blocks, weights[1], precision=highest)
        + bias_real
    )
    new_imag = (
        jnp.einsum("...ni,nio->...no", real_blocks, weights[1], precision=highest)
        + jnp.einsum("...ni,nio->...no", imag_blocks, weights[0], precision=highest)
        + bias_imag
    )
    return (
        new_real.reshape(leading + (blocks * width_block,)),
        new_imag.reshape(leading + (blocks * width_block,)),
    )


def spectral_mlp(spec_real, spec_imag, spec_one, bias_one, spec_two, bias_two):
    inner_real, inner_imag = block_mix(spec_real, spec_imag, spec_one, bias_one)
    return block_mix(smooth_gate(inner_real), smooth_gate(inner_imag), spec_two, bias_two)


def wave_tables(length, total_modes):
    positions = jnp.arange(length, dtype=jnp.int32)
    frequency = jnp.arange(total_modes, dtype=jnp.int32)
    phases = positions[:, None] * frequency[None, :] % length
    angles = phases.astype(jnp.float32) * (2.0 * math.pi / length)
    factor = 1.0 / math.sqrt(length)
    return (jnp.cos(angles) * factor, jnp.sin(angles) * factor)


def meridian_apply(table, field):
    return jnp.einsum("hk,bhmd->bkmd", table, field, precision=highest)


def meridian_forward(real_part, imag_part, merid_cos, merid_sin):
    new_real = meridian_apply(merid_cos, real_part) + meridian_apply(merid_sin, imag_part)
    new_imag = meridian_apply(merid_cos, imag_part) - meridian_apply(merid_sin, real_part)
    return (new_real, new_imag)


def meridian_inverse(real_part, imag_part, merid_cos, merid_sin):
    new_real = meridian_apply(merid_cos, real_part) - meridian_apply(merid_sin, imag_part)
    new_imag = meridian_apply(merid_cos, imag_part) + meridian_apply(merid_sin, real_part)
    return (new_real, new_imag)


def zonal_project(field, table):
    return jnp.einsum("brwd,wk->brkd", field, table, precision=highest)


def zonal_expand(field, table):
    return jnp.einsum("brkd,wk->brwd", field, table, precision=highest)


def local(
    stash,
    piece_map,
    gain_one,
    spec_one,
    bias_one,
    spec_two,
    bias_two,
    gain_two,
    fc_one,
    bias_fc,
    fc_two,
    cotangent,
):
    samples, lat_rows, lon_cells, model_width = cotangent.shape
    space_ranks = lax.axis_size("space")
    lat_total = lat_rows * space_ranks
    tokens = samples * lat_rows * lon_cells
    arrived = lax.all_to_all(stash, "space", split_axis=1, concat_axis=0, tiled=True)
    ordering = jnp.argsort(piece_map[:, 0])
    placed = jnp.take(arrived[:, 0], ordering, axis=0)
    inputs = jnp.transpose(placed, (1, 0, 2)).reshape(samples, lat_rows, lon_cells, model_width)
    base_field = inputs.astype(jnp.float32)
    zonal_cos, zonal_sin = wave_tables(lon_cells, KW)
    doubling = jnp.where(jnp.arange(KW) == 0, 1.0, 2.0).astype(jnp.float32)
    back_cos = zonal_cos * doubling
    back_sin = zonal_sin * doubling
    merid_cos, merid_sin = wave_tables(lat_total, lat_total)
    normed, pull_one = jax.vjp(layer_norm, base_field, gain_one)
    zonal_real = zonal_project(normed, zonal_cos)
    zonal_imag = -zonal_project(normed, zonal_sin)
    modes_real, modes_imag = in_one_piece((zonal_real, zonal_imag), "space", 2, 1, 0)
    spec_real, spec_imag = meridian_forward(modes_real, modes_imag, merid_cos, merid_sin)
    mixed_spec, pull_mix = jax.vjp(
        spectral_mlp, spec_real, spec_imag, spec_one, bias_one, spec_two, bias_two
    )
    back_real, back_imag = meridian_inverse(mixed_spec[0], mixed_spec[1], merid_cos, merid_sin)
    rows_real, rows_imag = in_one_piece((back_real, back_imag), "space", 1, 2, 0)
    spatial = zonal_expand(rows_real, back_cos) - zonal_expand(rows_imag, back_sin)
    mixed_field = base_field + normed + spatial
    normed_two, pull_two = jax.vjp(layer_norm, mixed_field, gain_two)
    normed_flat = normed_two.astype(jnp.bfloat16).reshape(tokens, model_width)
    hidden_pre = jnp.dot(normed_flat, fc_one, preferred_element_type=jnp.float32) + bias_fc
    active, pull_gate = jax.vjp(smooth_gate, hidden_pre)
    active_flat = active.astype(jnp.bfloat16)
    upstream = cotangent.reshape(tokens, model_width)
    grad_active = jnp.einsum("td,fd->tf", upstream, fc_two, preferred_element_type=jnp.float32)
    grad_hidden = pull_gate(grad_active)[0]
    grad_hidden_flat = grad_hidden.astype(jnp.bfloat16)
    grad_normed_two = jnp.einsum(
        "tf,df->td", grad_hidden_flat, fc_one, preferred_element_type=jnp.float32
    )
    term_one = jnp.einsum(
        "td,tf->df", normed_flat, grad_hidden_flat, preferred_element_type=jnp.float32
    )
    term_two = jnp.einsum("td,tf->df", upstream, active_flat, preferred_element_type=jnp.float32)
    grad_mixed_norm, grad_gain_two = pull_two(grad_normed_two.reshape(mixed_field.shape))
    grad_mixed = cotangent.astype(jnp.float32) + grad_mixed_norm
    grad_back_real = zonal_project(grad_mixed, back_cos)
    grad_back_imag = -zonal_project(grad_mixed, back_sin)
    grad_modes_real, grad_modes_imag = in_one_piece(
        (grad_back_real, grad_back_imag), "space", 2, 1, 0
    )
    grad_out_real, grad_out_imag = meridian_forward(
        grad_modes_real, grad_modes_imag, merid_cos, merid_sin
    )
    pulled = pull_mix((grad_out_real, grad_out_imag))
    grad_merid_real, grad_merid_imag = meridian_inverse(pulled[0], pulled[1], merid_cos, merid_sin)
    grad_rows_real, grad_rows_imag = in_one_piece(
        (grad_merid_real, grad_merid_imag), "space", 1, 2, 0
    )
    grad_normed = (
        grad_mixed
        + zonal_expand(grad_rows_real, zonal_cos)
        - zonal_expand(grad_rows_imag, zonal_sin)
    )
    grad_base, grad_gain_one = pull_one(grad_normed)
    grad_input = grad_mixed + grad_base
    bias_sum = jnp.sum(grad_hidden, axis=0)
    out_sum = jnp.sum(cotangent, axis=(0, 1, 2), dtype=jnp.float32)
    totals = lax.psum(
        (
            grad_gain_one,
            grad_gain_two,
            pulled[2],
            pulled[3],
            pulled[4],
            pulled[5],
            bias_sum,
            out_sum,
        ),
        ("dp", "space"),
    )
    paired = side_by_side((term_one, term_two), "dp", 1, 0)
    summed = side_by_side((paired[0], paired[1]), "space", 1, 0)
    grad_scale = 1.0 / math.sqrt(samples * lax.axis_size("dp") * lat_total * lon_cells)
    return (
        grad_input,
        summed[0] * grad_scale,
        (summed[1] * grad_scale).T,
        totals[6] * grad_scale,
        totals[7] * grad_scale,
        totals[0] * grad_scale,
        totals[1] * grad_scale,
        totals[2] * grad_scale,
        totals[3] * grad_scale,
        totals[4] * grad_scale,
        totals[5] * grad_scale,
    )


def solution(mesh):
    placed = (
        P("space", None, "dp", None),
        P(None, "space"),
        P(),
        P(),
        P(),
        P(),
        P(),
        P(),
        P(),
        P(),
        P(),
        P("dp", "space", None, None),
    )
    return jax.shard_map(
        local,
        mesh=mesh,
        in_specs=placed,
        out_specs=(
            P("dp", "space", None, None),
            P(None, ("dp", "space")),
            P(("dp", "space"), None),
            P(),
            P(),
            P(),
            P(),
            P(),
            P(),
            P(),
            P(),
        ),
        check_vma=False,
    )
```

profile of v0, /device:TPU:1, one launch (start us, length us, event | category | flops | bytes accessed | tf_op | source)
XLA Modules:
  0.0 582.4 jit_solution(12047435370016026344)
XLA Ops:
  8.0 12.5 %all-to-all-start = ((bf16[1,64,2,2160]{3,2,0,1:T(2,128)(2,1)}), bf16[1,64,2,2160]{3,2,0,1:T(2,128)(2,1)S(1)}, u32[]{:S(2)}, u32[]{:S(2)}) async-start(bf16[1,64,2,2160]{3,2,0,1:T(2,128)(2,1)} %bitcast.618), calls=%async_computation | async-start | bytes 1114112 | tf_op jit(solution)/shard_map/all_to_all | solution.py:122
  20.5 2.7 sort.17
  23.2 11.9 %all-to-all-done = bf16[1,64,2,2160]{3,2,0,1:T(2,128)(2,1)S(1)} async-done(((bf16[1,64,2,2160]{3,2,0,1:T(2,128)(2,1)}), bf16[1,64,2,2160]{3,2,0,1:T(2,128)(2,1)S(1)}, u32[]{:S(2)}, u32[]{:S(2)}) %all-to-all-start) | async-done | bytes 552992 | tf_op jit(solution)/shard_map/all_to_all | solution.py:122
  35.1 1.7 gather_fusion
  37.5 1.1 reshape.693
  38.6 1.1 reshape.694
  40.4 1.3 fusion.29
  41.7 1.2 convolution_bitcast_fusion.4
  43.0 1.4 copy.66
  44.4 4.9 all-to-all-start.1
  49.6 16.6 %all-to-all-done.1 = f32[4,1,64,768]{3,0,1,2:T(4,128)S(1)} async-done(((f32[4,1,64,768]{3,0,1,2:T(4,128)}), f32[4,1,64,768]{3,0,1,2:T(4,128)S(1)}, u32[]{:S(2)}, u32[]{:S(2)}) %all-to-all-start.1) | async-done | bytes 786464 | tf_op jit(solution)/shard_map/all_to_all | solution.py:15
  66.5 1.4 fusion.151
  70.3 1.5 fusion.129
  71.8 1.4 fusion.27
  73.2 1.2 reshape.665
  74.4 1.9 convolution_subtract_fusion.2
  77.2 1.6 fusion.107
  80.3 1.1 copy.74
  81.4 1.2 reshape.669
  82.6 1.4 fusion.216
  84.0 1.8 fusion.19
  88.6 1.4 copy.75
  89.9 4.7 all-to-all-start.2
  94.9 6.5 %fusion.414 = f32[360,3072]{1,0:T(8,128)} fusion(bf16[360,768]{1,0:T(8,128)(2,1)S(1)} %reshape.661, bf16[3072,768]{1,0:T(8,128)(2,1)} %param.22), kind=kOutput, calls=%fused_computation.519 | convolution fusion | flops 1698693120 | bytes 9695232 | tf_op jit(solution)/shard_map/td,fd->tf/dot_general | solution.py:150
  101.4 10.4 %all-to-all-done.2 = f32[4,64,1,768]{3,0,2,1:T(4,128)S(1)} async-done(((f32[4,64,1,768]{3,0,2,1:T(4,128)}), f32[4,64,1,768]{3,0,2,1:T(4,128)S(1)}, u32[]{:S(2)}, u32[]{:S(2)}) %all-to-all-start.2) | async-done | bytes 786464 | tf_op jit(solution)/shard_map/all_to_all | solution.py:15
  112.1 1.3 fusion.131
  113.4 1.6 fusion.411
  116.4 8.3 %fusion.404 = (f32[3072]{0:T(1024)S(1)}, bf16[360,3072]{1,0:T(8,128)(2,1)S(1)}, f32[360,3072]{1,0:T(8,128)S(1)}) fusion(f32[360,3072]{1,0:T(8,128)} %fusion.414, f32[3072]{0:T(1024)S(1)} %copy-done.30, bf16[360,768]{1,0:T(8,128)(2,1)S(1)} %reshape.672, bf16[768,3072]{1,0:T(8,128)(2,1)} %param.20), kind=kOutput, calls=%fused_computation.510 | convolution fusion | flops 1723020288 | bytes 16355328 | tf_op jit(solution)/shard_map/dot_general | solution.py:146
  124.8 2.7 fusion.32
  127.4 2.8 convolution_bitcast_fusion
  130.3 7.0 %pad_maximum_fusion = f32[1536,3072]{1,0:T(8,128)} fusion(f32[768,3072]{1,0:T(8,128)S(1)} %convolution_bitcast_fusion, f32[768,3072]{1,0:T(8,128)S(1)} %fusion.32), kind=kLoop, calls=%fused_computation.1 | loop fusion | flops 4718592 | bytes 37748736 | tf_op jit(solution)/shard_map/concatenate | solution.py:27
  137.8 6.0 %fusion.34 = f32[360,768]{1,0:T(8,128)} fusion(bf16[768,3072]{1,0:T(8,128)(2,1)} %param.20, bf16[360,3072]{1,0:T(8,128)(2,1)} %copy-done.16), kind=kOutput, calls=%fused_computation.87 | convolution fusion | flops 1698693120 | bytes 8036352 | tf_op jit(solution)/shard_map/tf,df->td/dot_general | solution.py:153
  143.7 1.4 reshape.673
  147.2 1.7 convert_reduce_fusion
  148.9 1.1 fusion.24
  150.0 1.1 convolution_bitcast_fusion.3
  151.6 30.1 %all_to_all.20 = f32[4,1,64,768]{3,0,1,2:T(4,128)S(1)} all-to-all(f32[4,1,64,768]{3,0,1,2:T(4,128)S(1)} %copy.78), channel_id=1, replica_groups=mesh['dp'=2,'space'=64] {'space'}, dimensions={2} | all-to-all | bytes 1572864 | tf_op jit(solution)/shard_map/all_to_all | solution.py:15
  183.3 1.1 reshape.679
  185.0 1.4 fusion.413
  186.3 1.3 reshape.677
  187.6 2.2 convolution_bitcast_fusion.7
  189.9 1.1 convolution_bitcast_fusion.8
  191.2 1.1 convolution_bitcast_fusion.5
  192.3 1.2 convolution_bitcast_fusion.6
  196.6 2.0 fusion.70
  199.8 1.2 convolution_bitcast_fusion.9
  201.0 1.3 fusion.55
  205.8 149.3 %reduce-scatter.5.cloned.1.call-done = f32[1536,1536]{1,0:T(8,128)} async-done(((f32[1536,3072]{1,0:T(8,128)}), f32[1536,1536]{1,0:T(8,128)}) %reduce-scatter.5.cloned.1.call-update) | async-done | bytes 9437200 | tf_op jit(solution)/shard_map/reduce_scatter | solution.py:28
  355.0 9.7 %copy.108 = f32[1536,1536]{0,1:T(8,128)} copy(f32[1536,1536]{1,0:T(8,128)} %reduce-scatter.5.cloned.1.call-done) | data formatting | bytes 18874368
  364.7 1.9 fusion.140
  367.5 1.1 copy.85
  368.6 2.0 reshape.686
  370.6 1.9 fusion.146
  373.3 1.1 copy.84
  374.4 1.2 reshape.684
  378.3 1.4 copy.86
  379.7 12.2 %all-to-all-start.4 = ((f32[4,64,1,768]{3,0,2,1:T(4,128)}), f32[4,64,1,768]{3,0,2,1:T(4,128)S(1)}, u32[]{:S(2)}, u32[]{:S(2)}) async-start(f32[4,64,1,768]{3,0,2,1:T(4,128)} %copy.86), calls=%async_computation.4 | async-start | bytes 1572864 | tf_op jit(solution)/shard_map/all_to_all | solution.py:15
  392.0 1.6 fusion.48
  393.8 101.4 %all-reduce.16.cloned.1.call-done = (f32[2,8,96,96]{3,2,1,0:T(8,128)}, f32[2,8,96,96]{3,2,1,0:T(8,128)}) async-done(((f32[2,8,96,96]{3,2,1,0:T(8,128)}, f32[2,8,96,96]{3,2,1,0:T(8,128)}), (f32[2,8,96,96]{3,2,1,0:T(8,128)}, f32[2,8,96,96]{3,2,1,0:T(8,128)})) %all-reduce.16.cloned.1.call-update) | async-done | bytes 1179664 | tf_op jit(solution)/shard_map/psum | solution.py:184
  495.1 2.7 broadcast_multiply_fusion
  498.1 1.3 convolution_bitcast_fusion.1
  499.5 1.7 multiply_reduce_fusion.2
  502.2 2.1 copy.93
  504.3 64.9 %all-reduce.12 = (f32[3072]{0:T(1024)S(1)}, f32[768]{0:T(1024)S(1)}, f32[768]{0:T(1024)S(1)}, f32[768]{0:T(1024)S(1)}, f32[2,768]{1,0:T(2,128)S(1)}, /*index=5*/f32[2,768]{1,0:T(2,128)S(1)}) all-reduce(f32[3072]{0:T(1024)S(1)} %get-tuple-element.62, ...), channel_id=1, replica_groups=mesh['dp'=2,'space'=64] {'dp','space'}, use_global_device_ids=true, to_apply=%region_12.13 | all-reduce | flops 8448 | bytes 67584 | tf_op jit(solution)/shard_map/psum | solution.py:184
  (157 shorter events, 35.7 us)
Async XLA Ops:
  8.0 27.1 %all-to-all-start = ((bf16[1,64,2,2160]{3,2,0,1:T(2,128)(2,1)}), bf16[1,64,2,2160]{3,2,0,1:T(2,128)(2,1)S(1)}, u32[]{:S(2)}, u32[]{:S(2)}) async-start(bf16[1,64,2,2160]{3,2,0,1:T(2,128)(2,1)} %bitcast.618), calls=%async_computation | async-start | bytes 1114112 | tf_op jit(solution)/shard_map/all_to_all | solution.py:122
  39.7 0.7 copy-start.26
  44.4 4.9 copy-start.28
  44.4 5.0 copy-start.29
  44.4 21.8 %all-to-all-start.1 = ((f32[4,1,64,768]{3,0,1,2:T(4,128)}), f32[4,1,64,768]{3,0,1,2:T(4,128)S(1)}, u32[]{:S(2)}, u32[]{:S(2)}) async-start(f32[4,1,64,768]{3,0,1,2:T(4,128)} %copy.66), calls=%async_computation.1 | async-start | bytes 1572864 | tf_op jit(solution)/shard_map/all_to_all | solution.py:15
  68.5 1.1 copy-start.5
  69.7 2.1 copy-start.1
  69.7 2.1 copy-start.21
  74.4 4.4 copy-start.3
  74.4 1.9 copy-start.13
  76.4 0.8 copy-start.19
  79.4 4.5 copy-start.8
  80.3 3.7 copy-start.14
  85.8 1.2 copy-start.22
  89.9 4.7 copy-start.17
  89.9 21.8 %all-to-all-start.2 = ((f32[4,64,1,768]{3,0,2,1:T(4,128)}), f32[4,64,1,768]{3,0,2,1:T(4,128)S(1)}, u32[]{:S(2)}, u32[]{:S(2)}) async-start(f32[4,64,1,768]{3,0,2,1:T(4,128)} %copy.75), calls=%async_computation.2 | async-start | bytes 1572864 | tf_op jit(solution)/shard_map/all_to_all | solution.py:15
  94.6 260.4 %reduce-scatter.5.cloned.1.call-start = ((), (), s32[]{:S(2)}) async-start(), calls=%async_computation.7 | async-start | bytes 28311552 | tf_op jit(solution)/shard_map/reduce_scatter | solution.py:28
  94.9 6.5 %copy-start.23 = (bf16[360,768]{1,0:T(8,128)(2,1)}, bf16[360,768]{1,0:T(8,128)(2,1)S(1)}, u32[]{:S(2)}) copy-start(bf16[360,768]{1,0:T(8,128)(2,1)S(1)} %reshape.661) | copy-start | bytes 1658884
  115.0 0.7 copy-start.27
  115.7 0.7 copy-start.30
  124.7 2.7 copy-start.16
  124.7 2.7 copy-start.24
  137.3 357.9 %all-reduce.16.cloned.1.call-start = ((), (), s32[]{:S(2)}) async-start(), calls=%async_computation.9 | async-start | bytes 3145728 | tf_op jit(solution)/shard_map/psum | solution.py:184
  145.1 1.0 copy-start
  146.1 1.1 copy-start.18
  186.3 3.5 copy-start.9
  189.8 1.2 copy-start.20
  189.8 1.3 copy-start.25
  193.5 1.4 copy-start.15
  196.6 2.0 copy-start.4
  198.5 2.5 copy-start.10
  198.5 1.2 copy-start.2
  205.7 365.9 %reduce-scatter.7.cloned.1.call-start = ((), (), s32[]{:S(2)}) async-start(), calls=%async_computation.8 | async-start | bytes 9584640
  364.7 1.9 copy-start.6
  364.7 1.9 copy-start.11
  370.6 1.9 copy-start.7
  373.3 3.0 copy-start.12
  379.7 118.1 %all-to-all-start.4 = ((f32[4,64,1,768]{3,0,2,1:T(4,128)}), f32[4,64,1,768]{3,0,2,1:T(4,128)S(1)}, u32[]{:S(2)}, u32[]{:S(2)}) async-start(f32[4,64,1,768]{3,0,2,1:T(4,128)} %copy.86), calls=%async_computation.4 | async-start | bytes 1572864 | tf_op jit(solution)/shard_map/all_to_all | solution.py:15
Sparse Core Ops, SparseCore 0:
  137.4 217.5 reduce-scatter.4
  364.8 173.4 reduce-scatter.6
Sparse Core Ops, SparseCore 1:
  205.8 289.3 all-reduce.15
where the time goes:
time: 591 us; the launch traced here: 582 us
  waiting for transfers between devices  290 us (49%)
  blocking collectives  94.9 us (16%)
  matrix products  80.1 us (14%)
  local copies, waits for them, and re-layouts  42 us (7%)
  starting transfers between devices  34.8 us (6%)
  other arithmetic  24.1 us (4%)
  between operations  16.9 us (3%)
    reduce_scatter x1, waiting for transfers between devices, side_by_side(): result = lax.psum_scatter(both, axis, scatter_dimension=dim, tiled=True)  149 us
    psum x1, waiting for transfers between devices, local(): lax.psum((grad_gain_one, grad_gain_two, pulled[2], pulled[3], pulled[4],...  101 us
    psum x1, blocking collectives, local(): lax.psum((grad_gain_one, grad_gain_two, pulled[2], pulled[3], pulled[4],...  64.9 us
    all_to_all x1, blocking collectives, in_one_piece(): lax.all_to_all(both, axis, split_axis=split_dim, concat_axis=concat_dim,...  30.1 us
    all_to_all x3, waiting for transfers between devices, in_one_piece(): lax.all_to_all(both, axis, split_axis=split_dim, concat_axis=concat_dim,...  27 us
    all_to_all x3, starting transfers between devices, in_one_piece(): lax.all_to_all(both, axis, split_axis=split_dim, concat_axis=concat_dim,...  21.8 us
    unnamed x69, local copies, waits for them, and re-layouts  17 us
    dot_general x16, matrix products, meridian_apply(): return jnp.einsum('hk,bhmd->bkmd', table, field, precision=highest)  13.3 us
  transfers between devices with their start and end apart: 7, of which 5 were waited for; matrix products, arithmetic and copies ran while one was open for 14% of the time, Pallas kernels for 0%

commit v1 on v0

--- a/solution.py
+++ b/solution.py
@@ -181,7 +181,8 @@
     grad_input = grad_mixed + grad_base
     bias_sum = jnp.sum(grad_hidden, axis=0)
     out_sum = jnp.sum(cotangent, axis=(0, 1, 2), dtype=jnp.float32)
-    totals = lax.psum(
+    _supply_notes = lambda v0: lax.psum(lax.psum(v0, axis_name="space"), axis_name="dp")
+    totals = _supply_notes(
         (
             grad_gain_one,
             grad_gain_two,
@@ -191,8 +192,7 @@
             pulled[5],
             bias_sum,
             out_sum,
-        ),
-        ("dp", "space"),
+        )
     )
     paired = side_by_side((term_one, term_two), "dp", 1, 0)
     summed = side_by_side((paired[0], paired[1]), "space", 1, 0)

time: 591 us -> 1420 us (2.40)
  waiting for transfers between devices: 290 us -> 855 us
  blocking collectives: 94.9 us -> 323 us
  matrix products: 80.1 us -> 94.5 us
    psum x1 -> x2, waiting for transfers between devices: 101 us -> 797 us  [the longest x1 797 us: local(): lax.psum(v0, axis_name='space')]
    psum x1 -> x2, blocking collectives: 64.9 us -> 323 us  [the longest x1 317 us: local(): lax.psum(v0, axis_name='space')]
    reduce_scatter x1, waiting for transfers between devices: 149 us -> 0.03 us  [side_by_side(): result = lax.psum_scatter(both, axis, scatter_dimension=dim, tiled=True)]
    all_to_all x1 -> x0, blocking collectives: 30.1 us -> none  [in_one_piece(): lax.all_to_all(both, axis, split_axis=split_dim, concat_axis=concat_dim,...]
    all_to_all x3 -> x4, waiting for transfers between devices: 27 us -> 46.5 us  [in_one_piece(): lax.all_to_all(both, axis, split_axis=split_dim, concat_axis=concat_dim,...]
  transfers between devices with their start and end apart: 7 -> 9, of which waited for: 5 -> 5; matrix products, arithmetic and copies ran while one was open for 14% -> 6% of each run, Pallas kernels for 0% -> 0%
where the time goes in v1:
time: 1420 us; the launch traced here: 1400 us
  waiting for transfers between devices  855 us (60%)
  blocking collectives  323 us (23%)
  matrix products  94.5 us (7%)
  local copies, waits for them, and re-layouts  43.6 us (3%)
  starting transfers between devices  37.5 us (3%)
  other arithmetic  32.6 us (2%)
  between operations  16.6 us (1%)
    psum x1, waiting for transfers between devices, local(): lax.psum(v0, axis_name='space')  797 us
    psum x1, blocking collectives, local(): lax.psum(v0, axis_name='space')  317 us
    all_to_all x4, waiting for transfers between devices, in_one_piece(): lax.all_to_all(both, axis, split_axis=split_dim, concat_axis=concat_dim,...  46.5 us
  transfers between devices with their start and end apart: 9, of which 5 were waited for; matrix products, arithmetic and copies ran while one was open for 6% of the time, Pallas kernels for 0%

profile of v1, /device:TPU:1, one launch (start us, length us, event | category | flops | bytes accessed | tf_op | source)
XLA Modules:
  0.0 1402.6 jit_solution(7764050215067676864)
XLA Ops:
  8.0 12.5 all-to-all-start
  20.5 2.7 sort.17
  23.2 11.9 all-to-all-done
  35.1 1.7 gather_fusion
  37.5 1.1 reshape.693
  38.6 1.1 reshape.694
  40.4 1.3 fusion.29
  41.7 1.2 convolution_bitcast_fusion.4
  43.0 1.4 copy.66
  44.4 4.9 all-to-all-start.1
  49.6 16.6 %all-to-all-done.1 = f32[4,1,64,768]{3,0,1,2:T(4,128)S(1)} async-done(((f32[4,1,64,768]{3,0,1,2:T(4,128)}), f32[4,1,64,768]{3,0,1,2:T(4,128)S(1)}, u32[]{:S(2)}, u32[]{:S(2)}) %all-to-all-start.1) | async-done | bytes 786464 | tf_op jit(solution)/shard_map/all_to_all | solution.py:15
  66.5 1.4 fusion.151
  70.3 1.5 fusion.129
  71.8 1.4 fusion.27
  73.2 1.3 reshape.665
  76.6 1.6 fusion.107
  80.9 1.8 fusion.19
  85.6 1.4 copy.75
  87.0 4.7 all-to-all-start.2
  91.9 6.5 fusion.414
  98.4 10.4 all-to-all-done.2
  109.2 1.3 fusion.131
  110.5 1.6 fusion.411
  113.5 9.5 fusion.404
  123.0 1.4 copy-done.18
  124.4 5.2 fusion.34
  129.6 1.4 reshape.673
  133.1 1.7 convert_reduce_fusion
  134.8 1.1 fusion.24
  137.0 1.4 copy.78
  138.4 4.5 all-to-all-start.3
  143.2 8.2 fusion.32
  151.4 8.7 convolution_bitcast_fusion
  160.4 1.4 fusion.153
  162.4 1.4 fusion.413
  163.8 1.3 reshape.677
  165.1 2.9 convolution_bitcast_fusion.7
  168.1 1.9 convolution_bitcast_fusion.8
  170.0 1.4 fusion.412
  171.4 2.0 reshape.679
  173.4 2.4 convolution_bitcast_fusion.5
  175.8 1.4 convolution_bitcast_fusion.6
  178.9 1.9 fusion.70
  183.1 1.3 fusion.55
  186.8 1.4 pad_add_fusion
  188.3 14.4 %pad_maximum_fusion = f32[1536,3072]{1,0:T(8,128)} fusion(f32[768,3072]{1,0:T(8,128)} %convolution_bitcast_fusion, f32[768,3072]{1,0:T(8,128)} %fusion.32), kind=kLoop, calls=%fused_computation.1 | loop fusion | flops 4718592 | bytes 37748736 | tf_op jit(solution)/shard_map/concatenate | solution.py:27
  202.8 796.7 %all-reduce.19.cloned.1.call-done = (f32[2,8,96,96]{3,2,1,0:T(8,128)}, f32[2,8,96,96]{3,2,1,0:T(8,128)}) async-done(((f32[2,8,96,96]{3,2,1,0:T(8,128)}, f32[2,8,96,96]{3,2,1,0:T(8,128)}), (f32[2,8,96,96]{3,2,1,0:T(8,128)}, f32[2,8,96,96]{3,2,1,0:T(8,128)})) %all-reduce.19.cloned.1.call-update) | async-done | bytes 1179664 | tf_op jit(solution)/shard_map/psum | solution.py:184
  1000.0 9.7 copy.108
  1009.7 1.9 fusion.140
  1012.5 1.1 copy.85
  1013.6 2.0 reshape.686
  1015.6 1.9 fusion.146
  1018.3 1.1 copy.84
  1019.4 1.3 reshape.684
  1023.3 1.4 copy.86
  1024.7 10.2 all-to-all-start.4
  1035.0 1.6 fusion.48
  1036.8 19.5 %all-to-all-done.4 = f32[4,64,1,768]{3,0,2,1:T(4,128)S(1)} async-done(((f32[4,64,1,768]{3,0,2,1:T(4,128)}), f32[4,64,1,768]{3,0,2,1:T(4,128)S(1)}, u32[]{:S(2)}, u32[]{:S(2)}) %all-to-all-start.4) | async-done | bytes 786464 | tf_op jit(solution)/shard_map/all_to_all | solution.py:15
  1056.6 1.3 convolution_bitcast_fusion.1
  1057.9 1.7 multiply_reduce_fusion.2
  1060.6 2.1 copy.93
  1062.8 317.0 %all-reduce.12 = (f32[3072]{0:T(1024)S(1)}, f32[768]{0:T(1024)S(1)}, f32[768]{0:T(1024)S(1)}, f32[768]{0:T(1024)S(1)}, f32[2,768]{1,0:T(2,128)S(1)}, /*index=5*/f32[2,768]{1,0:T(2,128)S(1)}) all-reduce(f32[3072]{0:T(1024)S(1)} %get-tuple-element.70, f32[768]{0:T(1024)S(1)} %get-tuple-element.80, ...), channel_id=1, replica_groups=mesh['dp'=2,'space'=64] {'space'}, use_global_device_ids=true, to_apply=%region_12.13 | all-reduce | flops 8448 | bytes 67584 | tf_op jit(solution)/shard_map/psum | solution.py:184
  1379.8 5.6 all-reduce.14
  1388.9 2.2 broadcast_multiply_fusion.1
  (177 shorter events, 38.4 us)
Async XLA Ops:
  8.0 27.1 %all-to-all-start = ((bf16[1,64,2,2160]{3,2,0,1:T(2,128)(2,1)}), bf16[1,64,2,2160]{3,2,0,1:T(2,128)(2,1)S(1)}, u32[]{:S(2)}, u32[]{:S(2)}) async-start(bf16[1,64,2,2160]{3,2,0,1:T(2,128)(2,1)} %bitcast.618), calls=%async_computation | async-start | bytes 1114112 | tf_op jit(solution)/shard_map/all_to_all | solution.py:122
  39.7 0.7 copy-start.33
  44.4 4.9 copy-start.35
  44.4 5.1 copy-start.36
  44.4 21.8 %all-to-all-start.1 = ((f32[4,1,64,768]{3,0,1,2:T(4,128)}), f32[4,1,64,768]{3,0,1,2:T(4,128)S(1)}, u32[]{:S(2)}, u32[]{:S(2)}) async-start(f32[4,1,64,768]{3,0,1,2:T(4,128)} %copy.66), calls=%async_computation.1 | async-start | bytes 1572864 | tf_op jit(solution)/shard_map/all_to_all | solution.py:15
  68.5 1.1 copy-start.5
  69.7 2.1 copy-start.1
  69.7 2.1 copy-start.26
  73.2 1.3 copy-start.24
  74.5 3.7 copy-start.3
  74.5 1.3 copy-start.15
  75.8 2.4 copy-start.22
  78.9 2.0 copy-start.8
  79.7 1.2 copy-start.16
  87.0 4.7 copy-start.19
  87.0 21.8 %all-to-all-start.2 = ((f32[4,64,1,768]{3,0,2,1:T(4,128)}), f32[4,64,1,768]{3,0,2,1:T(4,128)S(1)}, u32[]{:S(2)}, u32[]{:S(2)}) async-start(f32[4,64,1,768]{3,0,2,1:T(4,128)} %copy.75), calls=%async_computation.2 | async-start | bytes 1572864 | tf_op jit(solution)/shard_map/all_to_all | solution.py:15
  91.9 6.5 copy-start.28
  112.1 0.7 copy-start.34
  112.8 0.7 copy-start.37
  113.5 9.5 copy-start.21
  123.0 1.4 copy-start.18
  131.0 1.0 copy-start
  132.0 1.1 copy-start.20
  138.4 21.7 %all-to-all-start.3 = ((f32[4,1,64,768]{3,0,1,2:T(4,128)}), f32[4,1,64,768]{3,0,1,2:T(4,128)S(1)}, u32[]{:S(2)}, u32[]{:S(2)}) async-start(f32[4,1,64,768]{3,0,1,2:T(4,128)} %copy.78), calls=%async_computation.3 | async-start | bytes 1572864 | tf_op jit(solution)/shard_map/all_to_all | solution.py:15
  143.0 856.5 %all-reduce.19.cloned.1.call-start = ((), (), s32[]{:S(2)}) async-start(), calls=%async_computation.9 | async-start | bytes 3145728 | tf_op jit(solution)/shard_map/psum | solution.py:184
  143.2 8.3 copy-start.29
  160.4 3.4 copy-start.13
  163.8 4.2 copy-start.9
  168.1 1.9 copy-start.14
  168.1 1.9 copy-start.25
  173.4 2.4 copy-start.30
  175.8 1.4 copy-start.17
  177.2 1.7 copy-start.23
  178.9 1.9 copy-start.4
  180.8 2.3 copy-start.10
  180.8 1.2 copy-start.2
  184.7 2.1 copy-start.31
  184.7 2.1 copy-start.32
  188.2 811.7 %reduce-scatter.5.cloned.1.call-start = ((), (), s32[]{:S(2)}) async-start(), calls=%async_computation.7 | async-start | bytes 28311552 | tf_op jit(solution)/shard_map/reduce_scatter | solution.py:28
  202.7 1186.2 %all-reduce.21.cloned.1.call-start = ((), (), s32[]{:S(2)}) async-start(), calls=%async_computation.10 | async-start | bytes 3145728 | tf_op jit(solution)/shard_map/psum | solution.py:184
  999.5 392.6 %reduce-scatter.7.cloned.1.call-start = ((), (), s32[]{:S(2)}) async-start(), calls=%async_computation.8 | async-start | bytes 9584640
  1009.7 1.9 copy-start.6
  1009.7 1.9 copy-start.11
  1015.6 1.9 copy-start.7
  1018.3 3.0 copy-start.12
  1024.7 31.5 %all-to-all-start.4 = ((f32[4,64,1,768]{3,0,2,1:T(4,128)}), f32[4,64,1,768]{3,0,2,1:T(4,128)S(1)}, u32[]{:S(2)}, u32[]{:S(2)}) async-start(f32[4,64,1,768]{3,0,2,1:T(4,128)} %copy.86), calls=%async_computation.4 | async-start | bytes 1572864 | tf_op jit(solution)/shard_map/all_to_all | solution.py:15
  1388.9 2.2 copy-start.27
Sparse Core Ops, SparseCore 0:
  188.4 811.0 all-reduce.18
  1009.8 170.9 reduce-scatter.6
Sparse Core Ops, SparseCore 1:
  202.8 217.0 reduce-scatter.4
  999.6 61.8 all-reduce.20
